TPU v7x, 512 devices: a whole 4x8x8 slice. The times are simulated.
512 devices in a mesh: doc: 4 (over x), topic: 16 (over z, core), vocab: 8 (over y).
Axes of the slice: x: 4, y: 8, z: 8, core: 2. Of those that a mesh axis runs over, the one named last changes fastest.
Arguments:
- doc_topics: bfloat16 [2048, 16384], P('doc', 'topic'), may hold values from 0 to 1, as said below
- word_logits: bfloat16 [2048, 16384], P('vocab', 'topic'), may hold values from -6 to 11
- log_norm: float32 [16384], P('topic'), may hold values from 12 to 16
- tile_doc: int32 [512], P(('doc', 'vocab')), may hold values from 0 to 3, as said below
- tile_word: int32 [512], P(('doc', 'vocab')), may hold values from 0 to 3
- word_counts: int32 [512, 64, 128], P(('doc', 'vocab')), may hold values from 0 to 3, as said below
Outputs:
- doc_topic_grad: float32 [2048, 16384], P('doc', ('topic', 'vocab'))
- word_logit_grad: bfloat16 [2048, 16384], P('vocab', 'topic')
Inputs may be any that keep to these rules, and one draw needn't show every extreme that they name: `doc_topics`: each document's row is a softmax over the 16384 topics. Within the 16 slots of one doc and vocab index pair no (tile_doc, tile_word) pair repeats. `word_counts`: A slot whose counts are all zero is empty; occupied slots come first in each pair's list, and in every draw some pair has all 16 slots occupied.
All inputs are finite; a program needn't handle non-finite values.
Results may differ from a plain program's by a relative error of at most 0.018.
Values may be sent and summed in bfloat16 or wider, within the bound.
A program may use at most 64 MiB of HBM per device.

v0:
```python
import jax
import jax.numpy as jnp
from jax import lax
from jax.sharding import PartitionSpec as P

tiles_per_step = 8


def on_device(doc_topics, word_logits, log_norm, tile_doc, tile_word, word_counts):
    tile_total, word_span, doc_span = word_counts.shape
    topic_width = doc_topics.shape[1]
    word_prob = jnp.exp(word_logits.astype(jnp.float32) - log_norm[None, :]).astype(jnp.bfloat16)
    topic_blocks = doc_topics.reshape(-1, doc_span, topic_width)
    prob_blocks = word_prob.reshape(-1, word_span, topic_width)
    doc_rows = topic_blocks[tile_doc]
    word_rows = prob_blocks[tile_word]
    word_part = word_rows
    doc_part = doc_rows
    rate_full = lax.psum(
        jnp.einsum("gwk,gdk->gwd", word_part, doc_part, preferred_element_type=jnp.float32).astype(
            jnp.bfloat16
        ),
        "topic",
    ).astype(jnp.float32)
    ratios = (word_counts.astype(jnp.float32) / (word_span * rate_full)).astype(jnp.bfloat16)

    def accumulate(state_pair, group_index):
        theta_acc, beta_acc = state_pair
        first_row = group_index * tiles_per_step
        ratio_part = lax.dynamic_slice_in_dim(ratios, first_row, tiles_per_step, 0)
        word_part = lax.dynamic_slice_in_dim(word_rows, first_row, tiles_per_step, 0)
        doc_part = lax.dynamic_slice_in_dim(doc_rows, first_row, tiles_per_step, 0)
        doc_index = lax.dynamic_slice_in_dim(tile_doc, first_row, tiles_per_step, 0)
        word_index = lax.dynamic_slice_in_dim(tile_word, first_row, tiles_per_step, 0)
        toward_theta = jnp.einsum(
            "gwd,gwk->gdk", ratio_part, word_part, preferred_element_type=jnp.float32
        )
        toward_beta = jnp.einsum(
            "gwd,gdk->gwk", ratio_part, doc_part, preferred_element_type=jnp.float32
        )
        return (
            (theta_acc.at[doc_index].add(toward_theta), beta_acc.at[word_index].add(toward_beta)),
            None,
        )

    initial = (
        jnp.zeros(topic_blocks.shape, jnp.float32),
        jnp.zeros(prob_blocks.shape, jnp.float32),
    )
    steps_all = jnp.arange(tile_total // tiles_per_step, dtype=jnp.int32)
    (theta_acc, beta_acc), _ = lax.scan(accumulate, initial, steps_all)
    theta_term = -theta_acc.reshape(doc_topics.shape)
    doc_topic_grad = lax.psum_scatter(
        theta_term.astype(jnp.bfloat16), "vocab", scatter_dimension=1, tiled=True
    ).astype(jnp.float32)
    beta_term = -word_prob.astype(jnp.float32) * beta_acc.reshape(word_prob.shape)
    word_logit_grad = lax.psum(beta_term.astype(jnp.bfloat16), "doc")
    return (doc_topic_grad, word_logit_grad)


def solution(mesh):
    placed = (
        P("doc", "topic"),
        P("vocab", "topic"),
        P("topic"),
        P(("doc", "vocab")),
        P(("doc", "vocab")),
        P(("doc", "vocab"), None, None),
    )
    return jax.shard_map(
        on_device,
        mesh=mesh,
        in_specs=placed,
        out_specs=(P("doc", ("topic", "vocab")), P("vocab", "topic")),
        check_vma=False,
    )
```

profile of v0, /device:TPU:8, one launch (start us, length us, event | category | flops | bytes accessed | tf_op | source)
XLA Modules:
  0.0 288.9 jit_solution(454875629672425945)
XLA Ops:
  7.2 0.7 compare_select_fusion.2
  8.6 2.0 exponential_convert_fusion
  10.6 1.7 gather_fusion
  12.4 2.8 gather_fusion.1
  15.1 4.4 %convolution_convert_fusion = bf16[16,64,128]{2,1,0:T(8,128)(2,1)} fusion(bf16[16,64,1024]{2,1,0:T(8,128)(2,1)S(1)} %gather_fusion, bf16[16,128,1024]{2,1,0:T(8,128)(2,1)} %gather_fusion.1), kind=kOutput, calls=%fused_computation.15 | convolution fusion | flops 268566528 | bytes 6553600 | tf_op jit(solution)/shard_map/gwk,gdk->gwd/dot_general | solution.py:20
  19.7 119.4 %all-reduce.3.cloned.1.call-done = bf16[16,64,128]{2,1,0:T(8,128)(2,1)} async-done(((bf16[16,64,128]{2,1,0:T(8,128)(2,1)}), bf16[16,64,128]{2,1,0:T(8,128)(2,1)}) %all-reduce.3.cloned.1.call-update) | async-done | bytes 262160 | tf_op jit(solution)/shard_map/psum | solution.py:19
  139.1 1.2 divide_convert_fusion
  140.3 1.1 broadcast_in_dim.20
  141.7 38.2 %while.12 = (s32[]{:T(128)}, f32[4,128,1024]{2,1,0:T(8,128)S(1)}, f32[4,64,1024]{2,1,0:T(8,128)}, s32[2]{0:T(128)S(1)}, s32[16]{0:T(128)S(1)}, /*index=5*/bf16[1...) while((s32[]{:T(128)}, f32[4,128,1024]{2,1,0:T(8,128)S(1)}, ...), condition=%wide.region_4.5_spmd, body=%wide.region_1.4_spmd.sunk | while | flops 270008384 | bytes 28576132 | solution.py:51
  143.0 3.3 %fusion.22 = f32[8,64,1024]{2,1,0:T(8,128)} fusion(bf16[16,128,1024]{2,1,0:T(8,128)(2,1)} %get-tuple-element.165, s32[]{:T(128)S(6)} %select_n.28, bf16[16,64,128]{2,1,0:T(8,128)(2,1)S(1)} %get-tuple-element.162), kind=kOutput, calls=%fused_computation.4.clone.1 | convolution fusion | flops 134217728 | bytes 4326400 | tf_op jit(solution)/shard_map/while/body/eval_jaxpr/gwd,gdk->gwk/dot_general | solution.py:38
  146.4 4.8 %scatter_fusion.1 = f32[4,64,1024]{2,1,0:T(8,128)} fusion(f32[4,64,1024]{2,1,0:T(8,128)} %get-tuple-element.146, s32[8]{0:T(128)S(1)} %get-tuple-element.130, f32[8,64,1024]{2,1,0:T(8,128)} %fusion.22), kind=kCustom, calls=%fused_computation.3.clone.1 | custom fusion | flops 524288 | bytes 6291488 | tf_op jit(solution)/shard_map/while/body/eval_jaxpr/scatter-add | solution.py:42
  151.1 3.9 %fusion.21 = f32[8,128,1024]{2,1,0:T(8,128)} fusion(bf16[16,64,1024]{2,1,0:T(8,128)(2,1)} %get-tuple-element.163, s32[]{:T(128)S(6)} %select_n.28, bf16[16,64,128]{2,1,0:T(8,128)(2,1)S(1)} %get-tuple-element.162), kind=kOutput, calls=%fused_computation.6.clone.1 | convolution fusion | flops 134217728 | bytes 5374976 | tf_op jit(solution)/shard_map/while/body/eval_jaxpr/gwd,gwk->gdk/dot_general | solution.py:35
  155.1 5.7 %scatter_fusion = f32[4,128,1024]{2,1,0:T(8,128)S(1)} fusion(f32[4,128,1024]{2,1,0:T(8,128)S(1)} %get-tuple-element.145, s32[8]{0:T(128)S(1)} %get-tuple-element.129, f32[8,128,1024]{2,1,0:T(8,128)} %fusion.21), kind=kCustom, calls=%fused_computation.2.clone.1 | custom fusion | flops 1048576 | bytes 12582944 | tf_op jit(solution)/shard_map/while/body/eval_jaxpr/scatter-add | solution.py:42
  162.2 3.3 %fusion.22 = f32[8,64,1024]{2,1,0:T(8,128)} fusion(bf16[16,128,1024]{2,1,0:T(8,128)(2,1)} %get-tuple-element.165, s32[]{:T(128)S(6)} %select_n.28, bf16[16,64,128]{2,1,0:T(8,128)(2,1)S(1)} %get-tuple-element.162), kind=kOutput, calls=%fused_computation.4.clone.1 | convolution fusion | flops 134217728 | bytes 4326400 | tf_op jit(solution)/shard_map/while/body/eval_jaxpr/gwd,gdk->gwk/dot_general | solution.py:38
  165.5 4.8 %scatter_fusion.1 = f32[4,64,1024]{2,1,0:T(8,128)} fusion(f32[4,64,1024]{2,1,0:T(8,128)} %get-tuple-element.146, s32[8]{0:T(128)S(1)} %get-tuple-element.130, f32[8,64,1024]{2,1,0:T(8,128)} %fusion.22), kind=kCustom, calls=%fused_computation.3.clone.1 | custom fusion | flops 524288 | bytes 6291488 | tf_op jit(solution)/shard_map/while/body/eval_jaxpr/scatter-add | solution.py:42
  170.3 3.9 %fusion.21 = f32[8,128,1024]{2,1,0:T(8,128)} fusion(bf16[16,64,1024]{2,1,0:T(8,128)(2,1)} %get-tuple-element.163, s32[]{:T(128)S(6)} %select_n.28, bf16[16,64,128]{2,1,0:T(8,128)(2,1)S(1)} %get-tuple-element.162), kind=kOutput, calls=%fused_computation.6.clone.1 | convolution fusion | flops 134217728 | bytes 5374976 | tf_op jit(solution)/shard_map/while/body/eval_jaxpr/gwd,gwk->gdk/dot_general | solution.py:35
  174.2 5.7 %scatter_fusion = f32[4,128,1024]{2,1,0:T(8,128)S(1)} fusion(f32[4,128,1024]{2,1,0:T(8,128)S(1)} %get-tuple-element.145, s32[8]{0:T(128)S(1)} %get-tuple-element.129, f32[8,128,1024]{2,1,0:T(8,128)} %fusion.21), kind=kCustom, calls=%fused_computation.2.clone.1 | custom fusion | flops 1048576 | bytes 12582944 | tf_op jit(solution)/shard_map/while/body/eval_jaxpr/scatter-add | solution.py:42
  180.0 1.3 negate_convert_fusion
  181.2 2.4 copy.8
  183.7 1.0 fusion.8
  184.8 39.5 %reduce-scatter.4.cloned.1.call-done = bf16[128,512]{1,0:T(8,128)(2,1)} async-done(((bf16[1024,512]{1,0:T(8,128)(2,1)}), bf16[128,512]{1,0:T(8,128)(2,1)}) %reduce-scatter.4.cloned.1.call-update) | async-done | bytes 131088
  224.3 1.0 copy.9
  226.0 54.5 %all-reduce.5.cloned.1.call-done = bf16[256,1024]{1,0:T(8,128)(2,1)} async-done(((bf16[256,1024]{1,0:T(8,128)(2,1)}), bf16[256,1024]{1,0:T(8,128)(2,1)}) %all-reduce.5.cloned.1.call-update) | async-done | bytes 524304 | tf_op jit(solution)/shard_map/psum | solution.py:57
  280.5 1.9 copy.23
  (30 shorter events, 3.2 us)
Async XLA Ops:
  7.2 5.2 %copy-start = (bf16[512,1024]{1,0:T(8,128)(2,1)S(1)}, bf16[512,1024]{1,0:T(8,128)(2,1)}, u32[]{:S(2)}) copy-start(bf16[512,1024]{1,0:T(8,128)(2,1)} %param.8) | copy-start | bytes 3145732
  7.2 131.9 %all-reduce.3.cloned.1.call-start = ((), (), s32[]{:S(2)}) async-start(), calls=%async_computation.1 | async-start | bytes 524288 | tf_op jit(solution)/shard_map/psum | solution.py:19
  12.4 2.8 copy-start.2
  19.6 204.7 %reduce-scatter.4.cloned.1.call-start = ((), (), s32[]{:S(2)}) async-start(), calls=%async_computation.3 | async-start | bytes 1179648
  19.7 122.0 %copy-start.5 = (s32[16]{0:T(128)S(1)}, s32[16]{0:T(128)}, u32[]{:S(2)}) copy-start(s32[16]{0:T(128)} %param.12) | copy-start | bytes 196
  19.7 122.0 %copy-start.6 = (s32[16]{0:T(128)S(1)}, s32[16]{0:T(128)}, u32[]{:S(2)}) copy-start(s32[16]{0:T(128)} %param.11) | copy-start | bytes 196
  181.2 2.5 copy-start.1
  181.2 2.5 copy-start.3
  181.2 2.5 copy-start.4
  183.6 96.8 %all-reduce.5.cloned.1.call-start = ((), (), s32[]{:S(2)}) async-start(), calls=%async_computation.2 | async-start | bytes 1048576 | tf_op jit(solution)/shard_map/psum | solution.py:57
Sparse Core Ops, SparseCore 0:
  19.7 119.3 all-reduce.2
  183.8 40.4 reduce-scatter.3
  227.3 53.1 all-reduce.4
where the time goes:
time: 290 us; the launch traced here: 289 us
  waiting for transfers between devices  213 us (73%)
  other arithmetic  28.8 us (10%)
  matrix products  19 us (7%)
  between operations  13.9 us (5%)
  local copies, waits for them, and re-layouts  12.3 us (4%)
    psum x1, waiting for transfers between devices, on_device(): lax.psum(jnp.einsum('gwk,gdk->gwd', word_part, doc_part, preferred_elemen...  119 us
    psum x1, waiting for transfers between devices, on_device(): word_logit_grad = lax.psum(beta_term.astype(jnp.bfloat16), 'doc')  54.5 us
    unnamed x4, waiting for transfers between devices  39.6 us
    scatter-add x2, other arithmetic, accumulate(): theta_acc.at[doc_index].add(toward_theta)  11.5 us
    scatter-add x2, other arithmetic, accumulate(): beta_acc.at[word_index].add(toward_beta)  9.54 us
    dot_general x2, matrix products, accumulate(): jnp.einsum('gwd,gwk->gdk', ratio_part, word_part, preferred_element_type=...  7.89 us
    dot_general x2, matrix products, accumulate(): jnp.einsum('gwd,gdk->gwk', ratio_part, doc_part, preferred_element_type=j...  6.67 us
  transfers between devices with their start and end apart: 3, of which 3 were waited for; matrix products, arithmetic and copies ran while one was open for 1% of the time, Pallas kernels for 0%

commit v1 on v0

--- a/solution.py
+++ b/solution.py
@@ -16,7 +16,12 @@
     word_rows = prob_blocks[tile_word]
     word_part = word_rows
     doc_part = doc_rows
-    rate_full = lax.psum(
+
+    def view_the_values(packet, a_name):
+        t_next = jnp.sum(lax.all_gather(packet, axis_name=a_name), axis=0)
+        return t_next
+
+    rate_full = view_the_values(
         jnp.einsum("gwk,gdk->gwd", word_part, doc_part, preferred_element_type=jnp.float32).astype(
             jnp.bfloat16
         ),

time: 290 us -> 221 us (0.76)
  waiting for transfers between devices: 213 us -> 143 us
    psum x1 -> x0, waiting for transfers between devices: 119 us -> none  [on_device(): lax.psum(jnp.einsum('gwk,gdk->gwd', word_part, doc_part, preferred_elemen...]
    all_gather x0 -> x1, waiting for transfers between devices: none -> 50.4 us  [view_the_values(): t_next = jnp.sum(lax.all_gather(packet, axis_name=a_name), axis=0)]
    reduce_sum x0 -> x1, other arithmetic: none -> 3.18 us  [view_the_values(): t_next = jnp.sum(lax.all_gather(packet, axis_name=a_name), axis=0)]
where the time goes in v1:
time: 221 us; the launch traced here: 220 us
  waiting for transfers between devices  143 us (65%)
  other arithmetic  30.9 us (14%)
  matrix products  19 us (9%)
  between operations  13.9 us (6%)
  local copies, waits for them, and re-layouts  12.3 us (6%)
    psum x1, waiting for transfers between devices, on_device(): word_logit_grad = lax.psum(beta_term.astype(jnp.bfloat16), 'doc')  54.5 us
    all_gather x1, waiting for transfers between devices, view_the_values(): t_next = jnp.sum(lax.all_gather(packet, axis_name=a_name), axis=0)  50.4 us
    unnamed x4, waiting for transfers between devices  37.7 us
    scatter-add x2, other arithmetic, accumulate(): theta_acc.at[doc_index].add(toward_theta)  11.5 us
    scatter-add x2, other arithmetic, accumulate(): beta_acc.at[word_index].add(toward_beta)  9.54 us
    dot_general x2, matrix products, accumulate(): jnp.einsum('gwd,gwk->gdk', ratio_part, word_part, preferred_element_type=...  7.88 us
    dot_general x2, matrix products, accumulate(): jnp.einsum('gwd,gdk->gwk', ratio_part, doc_part, preferred_element_type=j...  6.69 us
    unnamed x19, local copies, waits for them, and re-layouts  5.32 us
  transfers between devices with their start and end apart: 3, of which 3 were waited for; matrix products, arithmetic and copies ran while one was open for 1% of the time, Pallas kernels for 0%

profile of v1, /device:TPU:8, one launch (start us, length us, event | category | flops | bytes accessed | tf_op | source)
XLA Modules:
  0.0 220.1 jit_solution(5261364690088767394)
XLA Ops:
  7.2 0.7 compare_select_fusion.2
  8.6 2.0 exponential_convert_fusion
  10.6 1.7 gather_fusion
  12.4 2.8 %gather_fusion.1 = bf16[16,128,1024]{2,1,0:T(8,128)(2,1)} fusion(bf16[4,128,1024]{2,1,0:T(8,128)(2,1)S(1)} %bitcast.15, s32[1024]{0:T(1024)S(1)} %pad_clamp_fusion), kind=kCustom, calls=%fused_computation.1 | custom fusion | bytes 8388672 | tf_op jit(solution)/shard_map/gather | solution.py:15
  15.1 4.4 %convolution_convert_fusion = bf16[16,64,128]{2,1,0:T(8,128)(2,1)} fusion(bf16[16,64,1024]{2,1,0:T(8,128)(2,1)S(1)} %gather_fusion, bf16[16,128,1024]{2,1,0:T(8,128)(2,1)} %gather_fusion.1), kind=kOutput, calls=%fused_computation.15 | convolution fusion | flops 268566528 | bytes 6553600 | tf_op jit(solution)/shard_map/gwk,gdk->gwd/dot_general | solution.py:25
  19.7 50.4 %all-gather.3.cloned.1.call-done = bf16[256,64,128]{2,1,0:T(8,128)(2,1)} async-done(((bf16[16,64,128]{2,1,0:T(8,128)(2,1)}), bf16[256,64,128]{2,1,0:T(8,128)(2,1)}) %all-gather.3.cloned.1.call-update) | async-done | bytes 4194320 | tf_op jit(solution)/shard_map/all_gather | solution.py:21
  70.0 3.2 %reduce_sum.12 = bf16[16,64,128]{2,1,0:T(8,128)(2,1)S(1)} reduce(bf16[16,16,64,128]{3,2,1,0:T(8,128)(2,1)} %bitcast.18, bf16[]{:T(256)} %constant.7.clone.1), dimensions={0}, to_apply=%region_0.0 | reduce | flops 1966080 | bytes 4456450 | tf_op jit(solution)/shard_map/reduce_sum | solution.py:21
  73.4 1.1 broadcast_in_dim.20
  74.7 38.3 %while.12 = (s32[]{:T(128)}, f32[4,128,1024]{2,1,0:T(8,128)S(1)}, f32[4,64,1024]{2,1,0:T(8,128)}, s32[2]{0:T(128)S(1)}, s32[16]{0:T(128)S(1)}, /*index=5*/bf16[1...) while((s32[]{:T(128)}, f32[4,128,1024]{2,1,0:T(8,128)S(1)}, ...), condition=%wide.region_4.5_spmd, body=%wide.region_1.4_spmd.sunk | while | flops 270008384 | bytes 28576132 | solution.py:56
  76.1 3.3 %fusion.22 = f32[8,64,1024]{2,1,0:T(8,128)} fusion(bf16[16,128,1024]{2,1,0:T(8,128)(2,1)} %get-tuple-element.165, s32[]{:T(128)S(6)} %select_n.28, bf16[16,64,128]{2,1,0:T(8,128)(2,1)S(1)} %get-tuple-element.162), kind=kOutput, calls=%fused_computation.4.clone.1 | convolution fusion | flops 134217728 | bytes 4326400 | tf_op jit(solution)/shard_map/while/body/eval_jaxpr/gwd,gdk->gwk/dot_general | solution.py:43
  79.4 4.8 %scatter_fusion.1 = f32[4,64,1024]{2,1,0:T(8,128)} fusion(f32[4,64,1024]{2,1,0:T(8,128)} %get-tuple-element.146, s32[8]{0:T(128)S(1)} %get-tuple-element.130, f32[8,64,1024]{2,1,0:T(8,128)} %fusion.22), kind=kCustom, calls=%fused_computation.3.clone.1 | custom fusion | flops 524288 | bytes 6291488 | tf_op jit(solution)/shard_map/while/body/eval_jaxpr/scatter-add | solution.py:47
  84.2 3.9 %fusion.21 = f32[8,128,1024]{2,1,0:T(8,128)} fusion(bf16[16,64,1024]{2,1,0:T(8,128)(2,1)} %get-tuple-element.163, s32[]{:T(128)S(6)} %select_n.28, bf16[16,64,128]{2,1,0:T(8,128)(2,1)S(1)} %get-tuple-element.162), kind=kOutput, calls=%fused_computation.6.clone.1 | convolution fusion | flops 134217728 | bytes 5374976 | tf_op jit(solution)/shard_map/while/body/eval_jaxpr/gwd,gwk->gdk/dot_general | solution.py:40
  88.1 5.7 %scatter_fusion = f32[4,128,1024]{2,1,0:T(8,128)S(1)} fusion(f32[4,128,1024]{2,1,0:T(8,128)S(1)} %get-tuple-element.145, s32[8]{0:T(128)S(1)} %get-tuple-element.129, f32[8,128,1024]{2,1,0:T(8,128)} %fusion.21), kind=kCustom, calls=%fused_computation.2.clone.1 | custom fusion | flops 1048576 | bytes 12582944 | tf_op jit(solution)/shard_map/while/body/eval_jaxpr/scatter-add | solution.py:47
  95.2 3.3 %fusion.22 = f32[8,64,1024]{2,1,0:T(8,128)} fusion(bf16[16,128,1024]{2,1,0:T(8,128)(2,1)} %get-tuple-element.165, s32[]{:T(128)S(6)} %select_n.28, bf16[16,64,128]{2,1,0:T(8,128)(2,1)S(1)} %get-tuple-element.162), kind=kOutput, calls=%fused_computation.4.clone.1 | convolution fusion | flops 134217728 | bytes 4326400 | tf_op jit(solution)/shard_map/while/body/eval_jaxpr/gwd,gdk->gwk/dot_general | solution.py:43
  98.5 4.8 %scatter_fusion.1 = f32[4,64,1024]{2,1,0:T(8,128)} fusion(f32[4,64,1024]{2,1,0:T(8,128)} %get-tuple-element.146, s32[8]{0:T(128)S(1)} %get-tuple-element.130, f32[8,64,1024]{2,1,0:T(8,128)} %fusion.22), kind=kCustom, calls=%fused_computation.3.clone.1 | custom fusion | flops 524288 | bytes 6291488 | tf_op jit(solution)/shard_map/while/body/eval_jaxpr/scatter-add | solution.py:47
  103.3 3.9 %fusion.21 = f32[8,128,1024]{2,1,0:T(8,128)} fusion(bf16[16,64,1024]{2,1,0:T(8,128)(2,1)} %get-tuple-element.163, s32[]{:T(128)S(6)} %select_n.28, bf16[16,64,128]{2,1,0:T(8,128)(2,1)S(1)} %get-tuple-element.162), kind=kOutput, calls=%fused_computation.6.clone.1 | convolution fusion | flops 134217728 | bytes 5374976 | tf_op jit(solution)/shard_map/while/body/eval_jaxpr/gwd,gwk->gdk/dot_general | solution.py:40
  107.3 5.7 %scatter_fusion = f32[4,128,1024]{2,1,0:T(8,128)S(1)} fusion(f32[4,128,1024]{2,1,0:T(8,128)S(1)} %get-tuple-element.145, s32[8]{0:T(128)S(1)} %get-tuple-element.129, f32[8,128,1024]{2,1,0:T(8,128)} %fusion.21), kind=kCustom, calls=%fused_computation.2.clone.1 | custom fusion | flops 1048576 | bytes 12582944 | tf_op jit(solution)/shard_map/while/body/eval_jaxpr/scatter-add | solution.py:47
  113.0 1.3 negate_convert_fusion
  114.3 2.4 %copy.8 = bf16[512,1024]{0,1:T(8,128)(2,1)} copy(bf16[512,1024]{1,0:T(8,128)(2,1)} %bitcast.17) | data formatting | bytes 2097152
  116.8 1.0 fusion.8
  117.8 37.6 %reduce-scatter.4.cloned.1.call-done = bf16[128,512]{1,0:T(8,128)(2,1)} async-done(((bf16[1024,512]{1,0:T(8,128)(2,1)}), bf16[128,512]{1,0:T(8,128)(2,1)}) %reduce-scatter.4.cloned.1.call-update) | async-done | bytes 131088
  155.5 1.0 copy.9
  157.2 54.5 %all-reduce.2.cloned.1.call-done = bf16[256,1024]{1,0:T(8,128)(2,1)} async-done(((bf16[256,1024]{1,0:T(8,128)(2,1)}), bf16[256,1024]{1,0:T(8,128)(2,1)}) %all-reduce.2.cloned.1.call-update) | async-done | bytes 524304 | tf_op jit(solution)/shard_map/psum | solution.py:62
  211.7 1.9 copy.22
  (33 shorter events, 3.3 us)
Async XLA Ops:
  7.2 5.2 %copy-start = (bf16[512,1024]{1,0:T(8,128)(2,1)S(1)}, bf16[512,1024]{1,0:T(8,128)(2,1)}, u32[]{:S(2)}) copy-start(bf16[512,1024]{1,0:T(8,128)(2,1)} %param.8) | copy-start | bytes 3145732
  7.2 62.8 %all-gather.3.cloned.1.call-start = ((), (), s32[]{:S(2)}) async-start(), calls=%async_computation.2 | async-start | bytes 4456448 | tf_op jit(solution)/shard_map/all_gather | solution.py:21
  12.4 2.8 %copy-start.2 = (bf16[16,64,1024]{2,1,0:T(8,128)(2,1)}, bf16[16,64,1024]{2,1,0:T(8,128)(2,1)S(1)}, u32[]{:S(2)}) copy-start(bf16[16,64,1024]{2,1,0:T(8,128)(2,1)S(1)} %gather_fusion) | copy-start | bytes 6291460
  19.6 135.9 %reduce-scatter.4.cloned.1.call-start = ((), (), s32[]{:S(2)}) async-start(), calls=%async_computation.3 | async-start | bytes 1179648
  70.0 3.2 %copy-start.4 = (s32[16,64,128]{2,1,0:T(8,128)S(1)}, s32[16,64,128]{2,1,0:T(8,128)}, u32[]{:S(2)}) copy-start(s32[16,64,128]{2,1,0:T(8,128)} %param.13) | copy-start | bytes 1572868
  73.2 1.5 copy-start.6
  73.2 1.5 copy-start.7
  114.3 2.5 %copy-start.1 = (f32[4,64,1024]{2,1,0:T(8,128)S(1)}, f32[4,64,1024]{2,1,0:T(8,128)}, u32[]{:S(2)}) copy-start(f32[4,64,1024]{2,1,0:T(8,128)} %get-tuple-element.51) | copy-start | bytes 3145732
  114.3 2.5 %copy-start.3 = (bf16[256,1024]{1,0:T(8,128)(2,1)S(1)}, bf16[256,1024]{1,0:T(8,128)(2,1)}, u32[]{:S(2)}) copy-start(bf16[256,1024]{1,0:T(8,128)(2,1)} %param.9) | copy-start | bytes 1572868
  114.3 2.5 %copy-start.5 = (f32[1024]{0:T(1024)S(1)}, f32[1024]{0:T(1024)}, u32[]{:S(2)}) copy-start(f32[1024]{0:T(1024)} %param.10) | copy-start | bytes 12292
  116.7 95.0 %all-reduce.2.cloned.1.call-start = ((), (), s32[]{:S(2)}) async-start(), calls=%async_computation.1 | async-start | bytes 1048576 | tf_op jit(solution)/shard_map/psum | solution.py:62
Sparse Core Ops, SparseCore 0:
  19.7 50.2 all-gather.2
  116.8 38.6 reduce-scatter.3
  158.4 53.2 all-reduce.1
